TPU v7x, 32 devices: a whole 2x2x4 slice. The times are simulated.
32 devices in a mesh: tm: 4 (over x, core), tile: 8 (over z, y).
Axes of the slice: x: 2, y: 2, z: 4, core: 2. Of those that a mesh axis runs over, the one named last changes fastest.
Arguments:
- pcs: float32 [2, 256], P(None, 'tm'), may hold values from -6 to 6
- st_eof: float32 [2, 120, 512], replicated, may hold values from -6 to 6
- spatial_eof: bfloat16 [2, 512, 64, 2048], P(None, 'tm', 'tile'), may hold values from -1 to 1
- land_sea: int32 [64, 2048], P('tile'), may hold values 0 or 1
Outputs:
- vorticity: float32 [256, 64, 2048], P('tm', 'tile')
- divergence: float32 [256, 64, 2048], P('tm', 'tile')
All inputs are finite; a program needn't handle non-finite values. No bound on the sum of `land_sea` on one device may be relied on, other than what follows from the above.
Results may differ from a plain program's by a relative error of at most 0.0041.
Values may be sent and summed in bfloat16 or wider, within the bound.
A program may use at most 128 MiB of HBM per device.

v0:
```python
import math
import jax
import jax.numpy as jnp
from jax import lax
from jax.sharding import PartitionSpec as P


def padded_2(block, sides, width):
    for axis, dim in sides:
        count = lax.axis_size(axis)
        forward = [(i, i + 1) for i in range(count - 1)]
        backward = [(target, source) for source, target in forward]
        low = lax.ppermute(
            lax.slice_in_dim(block, block.shape[dim] - width, None, axis=dim), axis, forward
        )
        high = lax.ppermute(lax.slice_in_dim(block, 0, width, axis=dim), axis, backward)
        block = jnp.concatenate([low, block, high], axis=dim)
    return block


def lagged_rc(series, st_eof, first, count):
    day_index = first + jnp.arange(count, dtype=jnp.int32)
    lag_steps = jnp.arange(st_eof.shape[1], dtype=jnp.int32)
    lag_index = day_index[:, None] - lag_steps[None, :]
    inside = lag_index >= 0
    safe_index = jnp.maximum(lag_index, 0)
    values_lag = jnp.where(inside[None], series[:, safe_index], 0.0)
    lag_total = st_eof.shape[0] * st_eof.shape[1]
    lagged = jnp.transpose(values_lag, (1, 0, 2)).reshape(count, lag_total)
    lagged_sums = jnp.dot(
        lagged,
        st_eof.reshape(lag_total, -1),
        precision=lax.Precision.HIGHEST,
        preferred_element_type=jnp.float32,
    )
    window_len = jnp.minimum(day_index + 1, st_eof.shape[1]).astype(jnp.float32)
    return lagged_sums / window_len[:, None]


def curl_div(east_pad, north_pad, latitude):
    cosine = jnp.cos(latitude)
    cos_east = east_pad * cosine[None, :, None]
    cos_north = north_pad * cosine[None, :, None]
    inner_east = east_pad[:, 1:-1]
    inner_north = north_pad[:, 1:-1]
    zonal_east = jnp.roll(inner_east, -1, axis=2) - jnp.roll(inner_east, 1, axis=2)
    zonal_north = jnp.roll(inner_north, -1, axis=2) - jnp.roll(inner_north, 1, axis=2)
    denominator = 2.0 * cosine[1:-1][None, :, None]
    vorticity = (zonal_north - (cos_east[:, 2:] - cos_east[:, :-2])) / denominator
    divergence = (zonal_east + (cos_north[:, 2:] - cos_north[:, :-2])) / denominator
    return (vorticity, divergence)


def shards(pcs, st_eof, spatial_eof, land_sea):
    day_dev = pcs.shape[1]
    all_pcs = lax.all_gather(pcs, "tm", axis=1, tiled=True)
    own_index = lax.axis_index("tm")
    lat_rows, lon_cells = land_sea.shape
    cell_count = lat_rows * lon_cells
    chan_share = spatial_eof.shape[1]
    local_eof = spatial_eof.reshape(2, chan_share, cell_count)
    own_rc = lagged_rc(all_pcs, st_eof, own_index * day_dev, day_dev).astype(jnp.bfloat16)
    fields = jnp.einsum(
        "tc,xcn->txn",
        own_rc,
        lax.all_gather(local_eof, "tm", axis=1, tiled=True),
        preferred_element_type=jnp.float32,
    )
    ocean_mask = land_sea.astype(jnp.float32)
    velocity = (
        (fields * ocean_mask.reshape(1, 1, cell_count))
        .astype(jnp.bfloat16)
        .reshape(day_dev, 2, lat_rows, lon_cells)
    )
    padded = padded_2(velocity, (("tile", 2),), 1)
    total_rows = lat_rows * lax.axis_size("tile")
    global_rows = (lax.axis_index("tile") * lat_rows).astype(jnp.float32) + jnp.arange(
        -1, lat_rows + 1, dtype=jnp.float32
    )
    latitude = (-70.0 + 140.0 * (global_rows + 0.5) / total_rows) * (math.pi / 180.0)
    vorticity, divergence = curl_div(
        padded[:, 0].astype(jnp.float32), padded[:, 1].astype(jnp.float32), latitude
    )
    return (vorticity * ocean_mask[None], divergence * ocean_mask[None])


def solution(mesh):
    return jax.shard_map(
        shards,
        mesh=mesh,
        in_specs=(P(None, "tm"), P(), P(None, "tm", "tile", None), P("tile", None)),
        out_specs=(P("tm", "tile", None), P("tm", "tile", None)),
        check_vma=False,
    )
```

profile of v0, /device:TPU:0, one launch (start us, length us, event | category | flops | bytes accessed | tf_op | source)
XLA Modules:
  0.0 354.6 jit_solution(9750223347867482415)
XLA Ops:
  7.2 0.0 copy-start
  7.2 0.0 all-gather.3.cloned.1.call-start
  7.2 13.6 %reshape.93 = bf16[2,128,16384]{2,1,0:T(8,128)(2,1)} reshape(bf16[2,128,8,2048]{3,2,1,0:T(8,128)(2,1)} %param.6) | data formatting | bytes 16777216 | tf_op jit(solution)/shard_map/reshape | solution.py:61
  20.8 0.0 copy-start.4
  20.8 0.0 all-gather.3.cloned.1.call-update
  20.8 0.0 copy-start.3
  20.8 0.1 subtract_maximum_fusion
  20.9 0.1 reshape.99
  21.0 0.4 copy-done.4
  21.5 6.0 %all-gather = f32[4,64,2]{1,2,0:T(2,128)S(1)} all-gather(f32[1,64,2]{1,2,0:T(2,128)S(1)} %bitcast.56), channel_id=1, replica_groups=mesh['tm'=4,'tile'=8] {'tm'}, dimensions={0}, use_global_device_ids=true | all-gather | bytes 2560 | tf_op jit(solution)/shard_map/all_gather | solution.py:56
  27.5 0.1 copy.8
  27.6 14.9 %gather_fusion = f32[7680,2]{1,0:T(8,128)} fusion(f32[2,256]{0,1:T(8,128)S(1)} %bitcast.54, s32[8192]{0:T(1024)S(1)} %pad_clamp_fusion), kind=kCustom, calls=%fused_computation | custom fusion | bytes 153600 | tf_op jit(solution)/shard_map/gather | solution.py:27
  42.6 3.9 %copy.9 = f32[64,120,2]{1,0,2:T(8,128)S(1)} copy(f32[64,120,2]{2,1,0:T(8,128)} %bitcast.53) | data formatting | bytes 122880 | tf_op jit(solution)/shard_map/gather | solution.py:27
  46.4 0.0 copy-done.3
  46.5 0.1 subtract_compare_fusion
  46.6 0.0 copy-done
  46.6 0.4 fusion.11
  47.0 178.2 %all-gather.3.cloned.1.call-done = bf16[2,512,16384]{2,1,0:T(8,128)(2,1)} async-done(((bf16[2,128,16384]{2,1,0:T(8,128)(2,1)}), bf16[2,512,16384]{2,1,0:T(8,128)(2,1)}) %all-gather.3.cloned.1.call-update) | async-done | bytes 33554448 | tf_op jit(solution)/shard_map/all_gather | solution.py:66
  225.2 18.5 %fusion = bf16[64,2,16384]{2,0,1:T(8,128)(2,1)} fusion(bf16[64,512,1]{1,0,2:T(8,128)(2,1)S(1)} %fusion.11, bf16[2,512,16384]{2,1,0:T(8,128)(2,1)} %all-gather.3.cloned.1.call-done, f32[16384]{0:T(1024)S(1)} %bitcast.55), kind=kOutput, calls=%fused_computation.2 | convolution fusion | flops 2151677952 | bytes 37879808 | tf_op jit(solution)/shard_map/tc,xcn->txn/dot_general | solution.py:63
  243.7 5.0 %copy.17 = bf16[16,8,8,2048]{3,2,1,0:T(8,128)(2,1)S(1)} copy(bf16[16,8,8,2048]{3,1,2,0:T(8,128)(2,1)} %bitcast.50) | data formatting | bytes 8388608
  248.7 0.0 copy-start.2
  248.7 2.0 copy-done.2
  250.7 1.4 fusion.21
  252.1 0.3 copy.14
  252.4 3.4 collective-permute-start
  255.9 0.3 copy.15
  256.2 1.5 collective-permute-start.1
  257.7 0.1 multiply_cosine_fusion
  257.7 0.1 slice_multiply_fusion
  257.8 20.9 %collective-permute-done = bf16[64,2,1,2048]{3,0,2,1:T(8,128)(2,1)S(1)} collective-permute-done((bf16[64,2,1,2048]{3,0,2,1:T(8,128)(2,1)S(1)}, bf16[64,2,1,2048]{3,0,2,1:T(8,128)(2,1)S(1)}, u32[]{:S(2)}, u32[]{:S(2)}) %collective-permute-start) | collective-permute-done | bytes 524320 | tf_op jit(solution)/shard_map/ppermute | solution.py:13
  278.6 0.8 copy.12
  279.5 0.0 collective-permute-done.1
  279.5 0.8 copy.13
  280.3 8.5 %pad_maximum_fusion = bf16[64,2,10,2048]{3,2,0,1:T(8,128)(2,1)} fusion(bf16[64,2,1,2048]{3,2,0,1:T(2,128)(2,1)S(1)} %copy.13, bf16[64,2,8,2048]{3,2,0,1:T(8,128)(2,1)} %bitcast.52, bf16[64,2,1,2048]{3,2,0,1:T(2,128)(2,1)S(1)} %copy.12), kind=kLoop, calls=%fused_computation.3 | loop fusion | flops 15728640 | bytes 10485760 | tf_op jit(solution)/shard_map/concatenate | solution.py:17
  288.8 11.3 %fusion.7 = (f32[64,10,2048]{2,1,0:T(8,128)}, f32[64,10,2048]{2,1,0:T(8,128)}) fusion(bf16[64,2,10,2048]{3,2,0,1:T(8,128)(2,1)} %pad_maximum_fusion), kind=kLoop, calls=%fused_computation.13 | loop fusion | flops 2621440 | bytes 15728640 | tf_op jit(solution)/shard_map/convert_element_type | solution.py:82
  300.1 17.3 %fusion.18 = (f32[64,8,2047]{2,1,0:T(8,128)S(1)}, f32[64,8,2047]{2,1,0:T(8,128)}, f32[64,8,2047]{2,1,0:T(8,128)}, f32[64,8,2047]{2,1,0:T(8,128)}) fusion(f32[64,10,2048]{2,1,0:T(8,128)} %get-tuple-element.8, f32[64,10,2048]{2,1,0:T(8,128)} %get-tuple-element.9), kind=kLoop, calls=%fused_computation.38 | loop fusion | bytes 33538048 | tf_op jit(solution)/shard_map/jit(_roll_static)/slice | solution.py:46
  317.5 2.6 fusion.17
  320.1 9.3 %broadcast_multiply_fusion = (f32[64,10,2048]{2,1,0:T(8,128)}, f32[64,10,2048]{2,1,0:T(8,128)}) fusion(f32[10]{0:T(128)S(1)} %multiply_cosine_fusion, bf16[64,2,10,2048]{3,2,0,1:T(8,128)(2,1)} %pad_maximum_fusion), kind=kLoop, calls=%fused_computation.18 | loop fusion | flops 5242880 | bytes 15728680 | tf_op jit(solution)/shard_map/mul | solution.py:43
  329.4 0.0 copy-start.1
  329.4 18.3 %fusion.3 = (f32[64,8,2048]{2,1,0:T(8,128)}, f32[64,8,2048]{2,1,0:T(8,128)}) fusion(f32[64,10,2048]{2,1,0:T(8,128)} %get-tuple-element.2, f32[64,8,1]{2,1,0:T(8,128)} %get-tuple-element.5, f32[64,8,2047]{2,1,0:T(8,128)} %get-tuple-element.7, f32[64,8,2047]{2,1,0:T(8,128)S(1)} %get-tuple-element.6, f32[64,8,1]{2,1,0:T(8,128)S(1)} %get-tuple-element.4, ...), kind=kLoop, calls=%fused_computation.7 | loop fusion | flops 14680064 | bytes 42008608 | tf_op jit(solution)/shard_map/mul | solution.py:84
  347.7 0.0 copy-done.1
  (5 shorter events, 0.1 us)
Async XLA Ops:
  7.2 39.4 %copy-start = (f32[2,120,512]{2,1,0:T(8,128)S(1)}, f32[2,120,512]{2,1,0:T(8,128)}, u32[]{:S(2)}) copy-start(f32[2,120,512]{2,1,0:T(8,128)} %param.5) | copy-start | bytes 1474564
  7.2 218.0 %all-gather.3.cloned.1.call-start = ((), (), s32[]{:S(2)}) async-start(), calls=%async_computation | async-start | bytes 41943040 | tf_op jit(solution)/shard_map/all_gather | solution.py:66
  20.8 0.7 copy-start.4
  20.8 25.6 %copy-start.3 = (s32[8,2048]{1,0:T(8,128)S(1)}, s32[8,2048]{1,0:T(8,128)}, u32[]{:S(2)}) copy-start(s32[8,2048]{1,0:T(8,128)} %param.7) | copy-start | bytes 196612
  248.7 2.0 copy-start.2
  252.4 26.2 %collective-permute-start = (bf16[64,2,1,2048]{3,0,2,1:T(8,128)(2,1)S(1)}, bf16[64,2,1,2048]{3,0,2,1:T(8,128)(2,1)S(1)}, u32[]{:S(2)}, u32[]{:S(2)}) collective-permute-start(bf16[64,2,1,2048]{3,0,2,1:T(8,128)(2,1)S(1)} %copy.14), channel_id=1, source_target_pairs={{0,1},{1,2},{2,3},{3,4},{4,5},{5,6},{6,7},{8,9},{9,10},{10,11},{11... | collective-permute-start | bytes 1572872 | tf_op jit(solution)/shard_map/ppermute | solution.py:13
  256.2 23.3 %collective-permute-start.1 = (bf16[64,2,1,2048]{3,0,2,1:T(8,128)(2,1)S(1)}, bf16[64,2,1,2048]{3,0,2,1:T(8,128)(2,1)S(1)}, u32[]{:S(2)}, u32[]{:S(2)}) collective-permute-start(bf16[64,2,1,2048]{3,0,2,1:T(8,128)(2,1)S(1)} %copy.15), channel_id=1, source_target_pairs={{1,0},{2,1},{3,2},{4,3},{5,4},{6,5},{7,6},{9,8},{10,9},{11,10},{12... | collective-permute-start | bytes 1572872 | tf_op jit(solution)/shard_map/ppermute | solution.py:16
  329.4 18.3 %copy-start.1 = (f32[2,120,512]{2,1,0:T(8,128)S(1)}, f32[2,120,512]{2,1,0:T(8,128)}, u32[]{:S(2)}) copy-start(f32[2,120,512]{2,1,0:T(8,128)} %param.5) | copy-start | bytes 1474564
Sparse Core Ops, SparseCore 0:
  20.9 204.2 all-gather.2
where the time goes:
time: 355 us
  waiting for transfers between devices  199 us (56%)
  local copies, waits for them, and re-layouts  63.7 us (18%)
  other arithmetic  47.8 us (13%)
  matrix products  18.9 us (5%)
  between operations  14.2 us (4%)
  blocking collectives  6 us (2%)
  starting transfers between devices  4.92 us (1%)
    all_gather x1, waiting for transfers between devices, shards(): lax.all_gather(local_eof, 'tm', axis=1, tiled=True)  178 us
    ppermute x1, waiting for transfers between devices, padded_2(): lax.ppermute(lax.slice_in_dim(block, block.shape[dim] - width, None, axis...  20.9 us
    slice x2, local copies, waits for them, and re-layouts, curl_div(): jnp.roll(inner_east, 1, axis=2)  19.9 us
    gather x2, local copies, waits for them, and re-layouts, lagged_rc(): values_lag = jnp.where(inside[None], series[:, safe_index], 0.0)  18.8 us
    dot_general x1, matrix products, shards(): jnp.einsum('tc,xcn->txn', own_rc, lax.all_gather(local_eof, 'tm', axis=1,...  18.5 us
    mul x1, other arithmetic, shards(): return (vorticity * ocean_mask[None], divergence * ocean_mask[None])  18.3 us
    reshape x1, local copies, waits for them, and re-layouts, shards(): local_eof = spatial_eof.reshape(2, chan_share, cell_count)  13.6 us
    convert_element_type x1, other arithmetic, shards(): padded[:, 0].astype(jnp.float32)  11.3 us
  transfers between devices with their start and end apart: 3, of which 2 were waited for; matrix products, arithmetic and copies ran while one was open for 6% of the time, Pallas kernels for 0%

commit v1 on v0

--- a/solution.py
+++ b/solution.py
@@ -1,8 +1,33 @@
+import functools
 import math
 import jax
 import jax.numpy as jnp
 from jax import lax
 from jax.sharding import PartitionSpec as P
+
+
+def mark_digits(x_in, dim_k):
+    x_in = jnp.moveaxis(x_in, 0, dim_k)
+    w_next = x_in.shape
+    return x_in.reshape(*w_next[:dim_k], w_next[dim_k] * w_next[dim_k + 1], *w_next[dim_k + 2 :])
+
+
+def tell_cards(raw, axis_tag):
+    y2, latest = (lax.psum(1, axis_name=axis_tag), lax.axis_index(axis_tag))
+    d_next, u1 = (raw[None], 1)
+    while u1 < y2:
+        r1 = lax.ppermute(d_next, axis_name=axis_tag, perm=[(p, p ^ u1) for p in range(y2)])
+        z2 = latest & u1 == 0
+        d_next = jnp.concatenate([jnp.where(z2, d_next, r1), jnp.where(z2, r1, d_next)])
+        u1 *= 2
+    return d_next
+
+
+def stacks_all_find(x_local, page, dimension_no):
+    return mark_digits(tell_cards(x_local, page), dimension_no)
+
+
+lane_take = functools.partial(stacks_all_find, page="tm", dimension_no=1)
 
 
 def padded_2(block, sides, width):
@@ -61,10 +86,7 @@
     local_eof = spatial_eof.reshape(2, chan_share, cell_count)
     own_rc = lagged_rc(all_pcs, st_eof, own_index * day_dev, day_dev).astype(jnp.bfloat16)
     fields = jnp.einsum(
-        "tc,xcn->txn",
-        own_rc,
-        lax.all_gather(local_eof, "tm", axis=1, tiled=True),
-        preferred_element_type=jnp.float32,
+        "tc,xcn->txn", own_rc, lane_take(local_eof), preferred_element_type=jnp.float32
     )
     ocean_mask = land_sea.astype(jnp.float32)
     velocity = (

time: 355 us -> 602 us (1.70)
  blocking collectives: 6 us -> 361 us
  waiting for transfers between devices: 199 us -> 34.1 us
  other arithmetic: 47.8 us -> 109 us
  between operations: 14.2 us -> 1 us
    all_gather x1, blocking collectives: 6 us -> 361 us  [shards(): all_pcs = lax.all_gather(pcs, 'tm', axis=1, tiled=True)]
    all_gather x1 -> x0, waiting for transfers between devices: 178 us -> none  [shards(): lax.all_gather(local_eof, 'tm', axis=1, tiled=True)]
    concatenate x0 -> x2, other arithmetic: none -> 32 us  [tell_cards(): jnp.concatenate([jnp.where(z2, d_next, r1), jnp.where(z2, r1, d_next)])]
    select_n x0 -> x2, other arithmetic: none -> 28.9 us  [tell_cards(): jnp.where(z2, d_next, r1)]
    reshape x1 -> x0, local copies, waits for them, and re-layouts: 13.6 us -> none  [shards(): local_eof = spatial_eof.reshape(2, chan_share, cell_count)]
    another operation x0 -> x1, local copies, waits for them, and re-layouts: none -> 13.5 us  [tell_cards(): d_next, u1 = (raw[None], 1)]
    ppermute x0 -> x2, waiting for transfers between devices: none -> 13.1 us  [tell_cards(): lax.ppermute(d_next, axis_name=axis_tag, perm=[(p, p ^ u1) for p in range...]
    slice x0 -> x2, local copies, waits for them, and re-layouts: none -> 11.4 us  [curl_div(): jnp.roll(inner_north, 1, axis=2)]
  transfers between devices with their start and end apart: 3 -> 4, of which waited for: 2 -> 2; matrix products, arithmetic and copies ran while one was open for 6% -> 3% of each run, Pallas kernels for 0% -> 0%
where the time goes in v1:
time: 602 us; the launch traced here: 601 us
  blocking collectives  361 us (60%)
  other arithmetic  109 us (18%)
  local copies, waits for them, and re-layouts  67.9 us (11%)
  waiting for transfers between devices  34.1 us (6%)
  matrix products  18.9 us (3%)
  starting transfers between devices  8.52 us (1%)
    all_gather x1, blocking collectives, shards(): all_pcs = lax.all_gather(pcs, 'tm', axis=1, tiled=True)  361 us
    concatenate x2, other arithmetic, tell_cards(): jnp.concatenate([jnp.where(z2, d_next, r1), jnp.where(z2, r1, d_next)])  32 us
    select_n x2, other arithmetic, tell_cards(): jnp.where(z2, d_next, r1)  28.9 us
    ppermute x1, waiting for transfers between devices, padded_2(): lax.ppermute(lax.slice_in_dim(block, block.shape[dim] - width, None, axis...  21 us
    dot_general x1, matrix products, shards(): jnp.einsum('tc,xcn->txn', own_rc, lane_take(local_eof), preferred_element...  18.5 us
    mul x1, other arithmetic, shards(): return (vorticity * ocean_mask[None], divergence * ocean_mask[None])  18.3 us
    gather x2, local copies, waits for them, and re-layouts, lagged_rc(): values_lag = jnp.where(inside[None], series[:, safe_index], 0.0)  17.6 us
    another operation x1, local copies, waits for them, and re-layouts, tell_cards(): d_next, u1 = (raw[None], 1)  13.5 us
  transfers between devices with their start and end apart: 4, of which 2 were waited for; matrix products, arithmetic and copies ran while one was open for 3% of the time, Pallas kernels for 0%

profile of v1, /device:TPU:0, one launch (start us, length us, event | category | flops | bytes accessed | tf_op | source)
XLA Modules:
  0.0 600.9 jit_solution(10615774104513090774)
XLA Ops:
  0.6 0.0 copy-start
  0.6 13.5 %broadcast_in_dim_reshape.3 = bf16[1,2,128,16384]{3,2,1,0:T(8,128)(2,1)} reshape(bf16[2,128,8,2048]{3,2,1,0:T(8,128)(2,1)} %param.6) | data formatting | bytes 16777216 | tf_op jit(solution)/shard_map/broadcast_in_dim;reshape | solution.py:17
  14.2 0.5 collective-permute-start
  14.7 13.1 %collective-permute-done = bf16[1,2,128,16384]{3,2,0,1:T(8,128)(2,1)} collective-permute-done((bf16[1,2,128,16384]{3,2,0,1:T(8,128)(2,1)}, bf16[1,2,128,16384]{3,2,0,1:T(8,128)(2,1)}, u32[]{:S(2)}, u32[]{:S(2)}) %collective-permute-start) | collective-permute-done | bytes 8388640 | tf_op jit(solution)/shard_map/ppermute | solution.py:19
  27.8 6.5 %broadcast_select_fusion.3 = (bf16[1,2,128,16384]{3,2,0,1:T(8,128)(2,1)S(1)}, bf16[1,2,128,16384]{3,2,0,1:T(8,128)(2,1)S(1)}) fusion(bf16[1,2,128,16384]{3,2,0,1:T(8,128)(2,1)} %collective-permute-done, pred[]{:T(512)S(6)} %eq.7, bf16[1,2,128,16384]{3,2,1,0:T(8,128)(2,1)} %broadcast_in_dim_reshape.3), kind=kLoop, calls=%fused_computation.9 | loop fusion | flops 8388608 | bytes 33554432 | tf_op jit(solution)/shard_map/jit(_where)/select_n | solution.py:21
  34.3 0.0 copy-start.2
  34.3 0.0 copy-start.3
  34.3 0.0 copy-start.6
  34.3 0.0 copy-start.5
  34.3 9.1 %pad_maximum_fusion.1 = bf16[2,2,128,16384]{3,2,0,1:T(8,128)(2,1)} fusion(bf16[1,2,128,16384]{3,2,0,1:T(8,128)(2,1)S(1)} %get-tuple-element.5, bf16[1,2,128,16384]{3,2,0,1:T(8,128)(2,1)S(1)} %get-tuple-element.4), kind=kLoop, calls=%fused_computation.4 | loop fusion | flops 8388608 | bytes 33554432 | tf_op jit(solution)/shard_map/concatenate | solution.py:21
  43.4 0.0 copy-done.2
  43.4 1.6 copy-done.3
  45.1 2.8 collective-permute-start.1
  47.9 0.1 subtract_maximum_fusion
  48.0 0.1 reshape.99
  48.1 0.0 copy-done.6
  48.1 361.5 %all-gather = f32[4,64,2]{1,2,0:T(2,128)S(1)} all-gather(f32[1,64,2]{1,2,0:T(2,128)S(1)} %bitcast.66), channel_id=1, replica_groups=mesh['tm'=4,'tile'=8] {'tm'}, dimensions={0}, use_global_device_ids=true | all-gather | bytes 2560 | tf_op jit(solution)/shard_map/all_gather | solution.py:81
  409.6 0.1 copy.14
  409.7 14.9 %gather_fusion = f32[7680,2]{1,0:T(8,128)} fusion(f32[2,256]{0,1:T(8,128)S(1)} %bitcast.64, s32[8192]{0:T(1024)S(1)} %pad_clamp_fusion), kind=kCustom, calls=%fused_computation | custom fusion | bytes 153600 | tf_op jit(solution)/shard_map/gather | solution.py:52
  424.7 2.7 copy.15
  427.4 0.0 copy-done.5
  427.4 0.1 subtract_compare_fusion
  427.5 0.0 copy-done
  427.5 0.4 fusion.11
  427.9 0.0 collective-permute-done.1
  428.0 22.4 %broadcast_select_fusion.1 = (bf16[2,2,128,16384]{3,2,0,1:T(8,128)(2,1)}, bf16[2,2,128,16384]{3,2,0,1:T(8,128)(2,1)}) fusion(bf16[2,2,128,16384]{3,2,0,1:T(8,128)(2,1)} %collective-permute-done.1, pred[]{:T(512)S(6)} %eq.6, bf16[1,2,128,16384]{3,2,0,1:T(8,128)(2,1)} %copy-done.3, bf16[1,2,128,16384]{3,2,0,1:T(8,128)(2,1)} %copy-done.2), kind=kLoop, calls=%fused_computation.6 | loop fusion | flops 25165824 | bytes 67108864 | tf_op jit(solution)/shard_map/jit(_where)/select_n | solution.py:21
  450.4 22.9 %pad_maximum_fusion = bf16[4,2,128,16384]{3,2,0,1:T(8,128)(2,1)} fusion(bf16[2,2,128,16384]{3,2,0,1:T(8,128)(2,1)} %get-tuple-element.3, bf16[2,2,128,16384]{3,2,0,1:T(8,128)(2,1)} %get-tuple-element.2), kind=kLoop, calls=%fused_computation.1 | loop fusion | flops 16777216 | bytes 67108864 | tf_op jit(solution)/shard_map/concatenate | solution.py:21
  473.3 18.5 %fusion = bf16[64,2,16384]{2,0,1:T(8,128)(2,1)} fusion(bf16[64,512,1]{1,0,2:T(8,128)(2,1)S(1)} %fusion.11, bf16[2,512,16384]{2,1,0:T(8,128)(2,1)} %bitcast.58, f32[16384]{0:T(1024)S(1)} %bitcast.65), kind=kOutput, calls=%fused_computation.3 | convolution fusion | flops 2151677952 | bytes 37879808 | tf_op jit(solution)/shard_map/tc,xcn->txn/dot_general | solution.py:88
  491.8 5.0 copy.26
  496.8 0.0 copy-start.4
  496.8 2.0 copy-done.4
  498.8 1.4 fusion.21
  500.3 0.3 copy.23
  500.6 3.7 collective-permute-start.2
  504.3 0.3 copy.24
  504.6 1.5 collective-permute-start.3
  506.1 0.1 multiply_cosine_fusion
  506.1 0.1 slice_multiply_fusion
  506.2 21.0 %collective-permute-done.2 = bf16[64,2,1,2048]{3,0,2,1:T(8,128)(2,1)S(1)} collective-permute-done((bf16[64,2,1,2048]{3,0,2,1:T(8,128)(2,1)S(1)}, bf16[64,2,1,2048]{3,0,2,1:T(8,128)(2,1)S(1)}, u32[]{:S(2)}, u32[]{:S(2)}) %collective-permute-start.2) | collective-permute-done | bytes 524320 | tf_op jit(solution)/shard_map/ppermute | solution.py:38
  527.2 0.8 copy.21
  528.0 0.0 collective-permute-done.3
  528.0 0.8 copy.22
  528.8 8.5 %pad_maximum_fusion.2 = bf16[64,2,10,2048]{3,2,0,1:T(8,128)(2,1)} fusion(bf16[64,2,1,2048]{3,2,0,1:T(2,128)(2,1)S(1)} %copy.22, bf16[64,2,8,2048]{3,2,0,1:T(8,128)(2,1)} %bitcast.62, bf16[64,2,1,2048]{3,2,0,1:T(2,128)(2,1)S(1)} %copy.21), kind=kLoop, calls=%fused_computation.7 | loop fusion | flops 15728640 | bytes 10485760 | tf_op jit(solution)/shard_map/concatenate | solution.py:42
  537.3 11.4 %fusion.7 = (f32[64,10,2048]{2,1,0:T(8,128)}, f32[64,10,2048]{2,1,0:T(8,128)}) fusion(bf16[64,2,10,2048]{3,2,0,1:T(8,128)(2,1)} %pad_maximum_fusion.2), kind=kLoop, calls=%fused_computation.19 | loop fusion | flops 2621440 | bytes 15728640 | tf_op jit(solution)/shard_map/convert_element_type | solution.py:104
  548.7 9.3 %fusion.20 = (f32[64,8,2047]{2,1,0:T(8,128)S(1)}, f32[64,8,2047]{2,1,0:T(8,128)}) fusion(f32[64,10,2048]{2,1,0:T(8,128)} %get-tuple-element.13), kind=kLoop, calls=%fused_computation.46 | loop fusion | bytes 16769024 | tf_op jit(solution)/shard_map/jit(_roll_static)/slice | solution.py:72
  558.0 2.0 fusion.19
  560.1 10.7 %fusion.18 = (f32[64,8,2047]{2,1,0:T(8,128)}, f32[64,8,2047]{2,1,0:T(8,128)}) fusion(f32[64,10,2048]{2,1,0:T(8,128)} %get-tuple-element.12), kind=kLoop, calls=%fused_computation.44 | loop fusion | bytes 16769024 | tf_op jit(solution)/shard_map/jit(_roll_static)/slice | solution.py:71
  570.7 2.1 fusion.17
  572.9 9.5 %broadcast_multiply_fusion = (f32[64,10,2048]{2,1,0:T(8,128)}, f32[64,10,2048]{2,1,0:T(8,128)}) fusion(f32[10]{0:T(128)S(1)} %multiply_cosine_fusion, bf16[64,2,10,2048]{3,2,0,1:T(8,128)(2,1)} %pad_maximum_fusion.2), kind=kLoop, calls=%fused_computation.24 | loop fusion | flops 5242880 | bytes 15728680 | tf_op jit(solution)/shard_map/mul | solution.py:68
  582.3 0.0 copy-start.1
  582.3 18.3 %fusion.3 = (f32[64,8,2048]{2,1,0:T(8,128)}, f32[64,8,2048]{2,1,0:T(8,128)}) fusion(f32[64,10,2048]{2,1,0:T(8,128)} %get-tuple-element.6, f32[64,8,1]{2,1,0:T(8,128)} %get-tuple-element.9, f32[64,8,2047]{2,1,0:T(8,128)} %get-tuple-element.11, f32[64,8,2047]{2,1,0:T(8,128)} %get-tuple-element.10, f32[64,8,1]{2,1,0:T(8,128)} %get-tuple-element.8, ...), kind=kLoop, calls=%fused_computation.13 | loop fusion | flops 14680064 | bytes 42008608 | tf_op jit(solution)/shard_map/mul | solution.py:106
  600.7 0.0 copy-done.1
  (4 shorter events, 0.1 us)
Async XLA Ops:
  0.6 426.9 %copy-start = (f32[2,120,512]{2,1,0:T(8,128)S(1)}, f32[2,120,512]{2,1,0:T(8,128)}, u32[]{:S(2)}) copy-start(f32[2,120,512]{2,1,0:T(8,128)} %param.5) | copy-start | bytes 1474564
  14.2 13.6 %collective-permute-start = (bf16[1,2,128,16384]{3,2,0,1:T(8,128)(2,1)}, bf16[1,2,128,16384]{3,2,0,1:T(8,128)(2,1)}, u32[]{:S(2)}, u32[]{:S(2)}) collective-permute-start(bf16[1,2,128,16384]{3,2,0,1:T(8,128)(2,1)} %bitcast.59), channel_id=1, source_target_pairs={{0,8},{8,0},{16,24},{24,16},{1,9},{9,1},{17,25},{25,17},{2,10},{10... | collective-permute-start | bytes 25165832 | tf_op jit(solution)/shard_map/ppermute | solution.py:19
  34.3 9.1 %copy-start.2 = (bf16[1,2,128,16384]{3,2,0,1:T(8,128)(2,1)}, bf16[1,2,128,16384]{3,2,0,1:T(8,128)(2,1)S(1)}, u32[]{:S(2)}) copy-start(bf16[1,2,128,16384]{3,2,0,1:T(8,128)(2,1)S(1)} %get-tuple-element.4) | copy-start | bytes 25165828
  34.3 10.8 %copy-start.3 = (bf16[1,2,128,16384]{3,2,0,1:T(8,128)(2,1)}, bf16[1,2,128,16384]{3,2,0,1:T(8,128)(2,1)S(1)}, u32[]{:S(2)}) copy-start(bf16[1,2,128,16384]{3,2,0,1:T(8,128)(2,1)S(1)} %get-tuple-element.5) | copy-start | bytes 25165828
  34.3 13.8 %copy-start.6 = (f32[2,64]{1,0:T(2,128)S(1)}, f32[2,64]{1,0:T(2,128)}, u32[]{:S(2)}) copy-start(f32[2,64]{1,0:T(2,128)} %param.4) | copy-start | bytes 1540
  34.3 393.0 %copy-start.5 = (s32[8,2048]{1,0:T(8,128)S(1)}, s32[8,2048]{1,0:T(8,128)}, u32[]{:S(2)}) copy-start(s32[8,2048]{1,0:T(8,128)} %param.7) | copy-start | bytes 196612
  45.1 382.9 %collective-permute-start.1 = (bf16[2,2,128,16384]{3,2,0,1:T(8,128)(2,1)}, bf16[2,2,128,16384]{3,2,0,1:T(8,128)(2,1)}, u32[]{:S(2)}, u32[]{:S(2)}) collective-permute-start(bf16[2,2,128,16384]{3,2,0,1:T(8,128)(2,1)} %pad_maximum_fusion.1), channel_id=1, source_target_pairs={{0,16},{8,24},{16,0},{24,8},{1,17},{9,25},{17,1},{25,9},{2,18},{10... | collective-permute-start | bytes 50331656 | tf_op jit(solution)/shard_map/ppermute | solution.py:19
  496.8 2.0 copy-start.4
  500.6 26.6 %collective-permute-start.2 = (bf16[64,2,1,2048]{3,0,2,1:T(8,128)(2,1)S(1)}, bf16[64,2,1,2048]{3,0,2,1:T(8,128)(2,1)S(1)}, u32[]{:S(2)}, u32[]{:S(2)}) collective-permute-start(bf16[64,2,1,2048]{3,0,2,1:T(8,128)(2,1)S(1)} %copy.23), channel_id=1, source_target_pairs={{0,1},{1,2},{2,3},{3,4},{4,5},{5,6},{6,7},{8,9},{9,10},{10,11},{11... | collective-permute-start | bytes 1572872 | tf_op jit(solution)/shard_map/ppermute | solution.py:38
  504.6 23.4 %collective-permute-start.3 = (bf16[64,2,1,2048]{3,0,2,1:T(8,128)(2,1)S(1)}, bf16[64,2,1,2048]{3,0,2,1:T(8,128)(2,1)S(1)}, u32[]{:S(2)}, u32[]{:S(2)}) collective-permute-start(bf16[64,2,1,2048]{3,0,2,1:T(8,128)(2,1)S(1)} %copy.24), channel_id=1, source_target_pairs={{1,0},{2,1},{3,2},{4,3},{5,4},{6,5},{7,6},{9,8},{10,9},{11,10},{12... | collective-permute-start | bytes 1572872 | tf_op jit(solution)/shard_map/ppermute | solution.py:41
  582.3 18.4 %copy-start.1 = (f32[2,120,512]{2,1,0:T(8,128)S(1)}, f32[2,120,512]{2,1,0:T(8,128)}, u32[]{:S(2)}) copy-start(f32[2,120,512]{2,1,0:T(8,128)} %param.5) | copy-start | bytes 1474564
